TPU v7x, 32 devices: a whole 2x2x4 slice. The times are simulated.
32 devices in a mesh: lat: 4 (over y, x), lon: 8 (over z, core).
Axes of the slice: x: 2, y: 2, z: 4, core: 2. Of those that a mesh axis runs over, the one named last changes fastest.
Arguments:
- right_side: float32 [512, 2048], P('lat', 'lon'), may hold values from -12 to 12
- diagonal: float32 [512, 2048], P('lat', 'lon'), may hold values from 0.2 to 2
- east_coef: float32 [512, 2048], P('lat', 'lon'), may hold values from 0.5 to 2
- north_coef: float32 [512, 2048], P('lat', 'lon'), may hold values from 0.5 to 2
- land_sea: int32 [512, 2048], P('lat', 'lon'), may hold values 0 or 1
- fold_partner: int32 [2048], P('lon'), may hold values from 0 to 2047, as said below
Outputs:
- solution_field: float32 [512, 2048], P('lat', 'lon')
- residual: float32 [512, 2048], P('lat', 'lon')
Inputs may be any that keep to these rules, and one draw needn't show every extreme that they name: fold_partner[fold_partner[i]] = i and fold_partner[i] != i for every column i, and fold_partner[i] // 256 = 7 - i // 256.
All inputs are finite; a program needn't handle non-finite values. No bound on the sum of `land_sea` on one device may be relied on, other than what follows from the above.
Results may differ from a plain program's by a relative error of at most 0.00019.
Values sent between devices are 32-bit elements; how exact they have to be, the bound alone decides.
A program may use at most 64 MiB of HBM per device.

v0:
```python
import jax
import jax.numpy as jnp
from jax import lax
from jax.sharding import PartitionSpec as P

ITERS = 4


def with_halo(cells, sides, width, closed):
    for axis, dim in sides:
        count = lax.axis_size(axis)
        ends = count if closed else count - 1
        head = lax.slice_in_dim(cells, 0, width, axis=dim)
        tail = lax.slice_in_dim(cells, cells.shape[dim] - width, cells.shape[dim], axis=dim)
        cells = jnp.concatenate(
            [
                lax.ppermute(tail, axis, [(i, (i + 1) % count) for i in range(ends)]),
                cells,
                lax.ppermute(head, axis, [((i + 1) % count, i) for i in range(ends)]),
            ],
            axis=dim,
        )
    return cells


def zonal_rim(values):
    return with_halo(values, (("lon", 1),), 1, True)


def meridional_rim(values):
    return with_halo(values, (("lat", 0),), 1, False)


def paired(residual, image):
    return lax.psum((jnp.sum(residual * residual), jnp.sum(residual * image)), ("lat", "lon"))


def local(right_side, diagonal, east_coef, north_coef, land_sea, fold_partner):
    row_count, col_count = right_side.shape
    ocean = land_sea.astype(jnp.float32)
    on_top = lax.axis_index("lat") == lax.axis_size("lat") - 1
    row_ids = lax.broadcasted_iota(jnp.int32, (row_count, col_count), 0)
    north_inner = jnp.where(on_top & (row_ids == row_count - 1), 0.0, north_coef)
    west_coef = zonal_rim(east_coef)[:, :col_count]
    south_coef = meridional_rim(north_inner)[:row_count]

    def neighbours(masked):
        across_lon = zonal_rim(masked)
        across_lat = meridional_rim(masked)
        return (
            across_lon[:, 2:],
            across_lon[:, :col_count],
            across_lat[2:],
            across_lat[:row_count],
        )

    def mirror_row(top_values):
        whole_row = lax.all_gather(top_values, "lon", axis=0, tiled=True)
        return jnp.take(whole_row, fold_partner, axis=0)

    top_coef = north_coef[row_count - 1]
    fold_coef = jnp.where(on_top, 0.5 * (top_coef + mirror_row(top_coef)), 0.0)

    def operate(surface):
        masked = ocean * surface
        east_vals, west_vals, north_vals, south_vals = neighbours(masked)
        spread = east_coef * (masked - east_vals) + west_coef * (masked - west_vals)
        spread = spread + north_inner * (masked - north_vals) + south_coef * (masked - south_vals)
        last_row = masked[row_count - 1]
        spread = spread.at[row_count - 1].add(fold_coef * (last_row - mirror_row(last_row)))
        return diagonal * surface + ocean * spread

    solution_field = jnp.zeros_like(right_side)
    residual = right_side
    image = operate(residual)
    norm_now, product = paired(residual, image)
    alpha = norm_now / product
    direction, along = (residual, image)
    for iteration in range(ITERS):
        solution_field = solution_field + alpha * direction
        residual = residual - alpha * along
        if iteration + 1 < ITERS:
            image = operate(residual)
            norm_next, product = paired(residual, image)
            ratio = norm_next / norm_now
            alpha = norm_next / (product - ratio * norm_next / alpha)
            direction = residual + ratio * direction
            along = image + ratio * along
            norm_now = norm_next
    return (solution_field, residual)


def solution(mesh):
    placed = (
        P("lat", "lon"),
        P("lat", "lon"),
        P("lat", "lon"),
        P("lat", "lon"),
        P("lat", "lon"),
        P("lon"),
    )
    return jax.shard_map(
        local,
        mesh=mesh,
        in_specs=placed,
        out_specs=(P("lat", "lon"), P("lat", "lon")),
        check_vma=False,
    )
```

profile of v0, /device:TPU:12, one launch (start us, length us, event | category | flops | bytes accessed | tf_op | source)
XLA Modules:
  0.0 291.9 jit_solution(6611212178361798222)
XLA Ops:
  1.8 3.4 %collective-permute-start.4 = (f32[1,256]{1,0:T(1,128)S(1)}, f32[1,256]{1,0:T(1,128)S(1)}, u32[]{:S(2)}, u32[]{:S(2)}) collective-permute-start(f32[1,256]{1,0:T(1,128)S(1)} %slice.255), channel_id=1, source_target_pairs={{0,8},{8,16},{16,24},{1,9},{9,17},{17,25},{2,10},{10,18},{18,26},{... | collective-permute-start | bytes 3080 | tf_op jit(solution)/shard_map/ppermute | solution.py:17
  5.3 3.3 %collective-permute-start.3 = (f32[1,256]{1,0:T(1,128)S(1)}, f32[1,256]{1,0:T(1,128)S(1)}, u32[]{:S(2)}, u32[]{:S(2)}) collective-permute-start(f32[1,256]{1,0:T(1,128)S(1)} %get-tuple-element.87), channel_id=1, source_target_pairs={{8,0},{16,8},{24,16},{9,1},{17,9},{25,17},{10,2},{18,10},{26,18},{... | collective-permute-start | bytes 3080 | tf_op jit(solution)/shard_map/ppermute | solution.py:19
  8.6 2.5 collective-permute-start.5
  12.1 10.8 %all-gather.1 = f32[1,2048]{1,0:T(1,128)S(1)} all-gather(f32[1,256]{1,0:T(1,128)S(1)} %get-tuple-element.88), channel_id=3, replica_groups=mesh['lat'=4,'lon'=8] {'lon'}, dimensions={1}, use_global_device_ids=true | all-gather | bytes 9216 | tf_op jit(solution)/shard_map/all_gather | solution.py:58
  22.9 10.2 %all-gather = f32[1,2048]{1,0:T(1,128)S(1)} all-gather(f32[1,256]{1,0:T(1,128)S(1)} %slice.214), channel_id=2, replica_groups=mesh['lat'=4,'lon'=8] {'lon'}, dimensions={1}, use_global_device_ids=true | all-gather | bytes 9216 | tf_op jit(solution)/shard_map/all_gather | solution.py:58
  33.1 1.7 gather_fusion
  34.8 1.7 gather_fusion.1
  37.0 3.3 %collective-permute-done.2 = f32[128,1]{1,0:T(8,128)S(1)} collective-permute-done((f32[128,1]{1,0:T(8,128)S(1)}, f32[128,1]{1,0:T(8,128)S(1)}, u32[]{:S(2)}, u32[]{:S(2)}) %collective-permute-start.2) | collective-permute-done | bytes 544 | tf_op jit(solution)/shard_map/ppermute | solution.py:17
  41.3 41.4 %all-reduce.3 = (f32[]{:T(128)}, f32[]{:T(128)}) all-reduce(f32[]{:T(128)} %get-tuple-element.58, f32[]{:T(128)} %get-tuple-element.57), channel_id=1, replica_groups=mesh['lat'=4,'lon'=8] {'lat','lon'}, use_global_device_ids=true, to_apply=%region_1.2 | all-reduce | flops 2 | bytes 16 | tf_op jit(solution)/shard_map/psum | solution.py:35
  84.1 8.3 %all-gather.2 = f32[1,2048]{1,0:T(1,128)S(1)} all-gather(f32[1,256]{1,0:T(1,128)S(1)} %get-tuple-element.84), channel_id=4, replica_groups=mesh['lat'=4,'lon'=8] {'lon'}, dimensions={1}, use_global_device_ids=true | all-gather | bytes 9216 | tf_op jit(solution)/shard_map/all_gather | solution.py:58
  92.4 3.8 %collective-permute-start.9 = (f32[1,256]{1,0:T(1,128)S(1)}, f32[1,256]{1,0:T(1,128)S(1)}, u32[]{:S(2)}, u32[]{:S(2)}) collective-permute-start(f32[1,256]{1,0:T(1,128)S(1)} %get-tuple-element.84), channel_id=1, source_target_pairs={{0,8},{8,16},{16,24},{1,9},{9,17},{17,25},{2,10},{10,18},{18,26},{... | collective-permute-start | bytes 3080 | tf_op jit(solution)/shard_map/ppermute | solution.py:17
  96.3 1.7 gather_fusion.2
  98.1 2.9 collective-permute-start.8
  102.5 1.9 collective-permute-done.6
  104.4 1.8 collective-permute-done.7
  107.2 42.0 %all-reduce.2 = (f32[]{:T(128)}, f32[]{:T(128)}) all-reduce(f32[]{:T(128)} %get-tuple-element.54, f32[]{:T(128)} %get-tuple-element.53), channel_id=1, replica_groups=mesh['lat'=4,'lon'=8] {'lat','lon'}, use_global_device_ids=true, to_apply=%region_5.7 | all-reduce | flops 2 | bytes 16 | tf_op jit(solution)/shard_map/psum | solution.py:35
  153.9 8.1 %all-gather.3 = f32[1,2048]{1,0:T(1,128)S(1)} all-gather(f32[1,256]{1,0:T(1,128)S(1)} %get-tuple-element.80), channel_id=5, replica_groups=mesh['lat'=4,'lon'=8] {'lon'}, dimensions={1}, use_global_device_ids=true | all-gather | bytes 9216 | tf_op jit(solution)/shard_map/all_gather | solution.py:58
  162.0 2.8 collective-permute-start.13
  164.9 1.7 gather_fusion.3
  166.6 3.9 %collective-permute-start.12 = (f32[1,256]{1,0:T(1,128)S(1)}, f32[1,256]{1,0:T(1,128)S(1)}, u32[]{:S(2)}, u32[]{:S(2)}) collective-permute-start(f32[1,256]{1,0:T(1,128)S(1)} %get-tuple-element.79), channel_id=1, source_target_pairs={{8,0},{16,8},{24,16},{9,1},{17,9},{25,17},{10,2},{18,10},{26,18},{... | collective-permute-start | bytes 3080 | tf_op jit(solution)/shard_map/ppermute | solution.py:19
  170.6 1.7 collective-permute-start.10
  172.3 1.9 collective-permute-done.10
  174.2 1.8 collective-permute-done.11
  177.0 40.9 %all-reduce.1 = (f32[]{:T(128)}, f32[]{:T(128)}) all-reduce(f32[]{:T(128)} %get-tuple-element.52, f32[]{:T(128)} %get-tuple-element.51), channel_id=1, replica_groups=mesh['lat'=4,'lon'=8] {'lat','lon'}, use_global_device_ids=true, to_apply=%region_9.11 | all-reduce | flops 2 | bytes 16 | tf_op jit(solution)/shard_map/psum | solution.py:35
  221.9 8.2 %all-gather.4 = f32[1,2048]{1,0:T(1,128)S(1)} all-gather(f32[1,256]{1,0:T(1,128)S(1)} %get-tuple-element.76), channel_id=6, replica_groups=mesh['lat'=4,'lon'=8] {'lon'}, dimensions={1}, use_global_device_ids=true | all-gather | bytes 9216 | tf_op jit(solution)/shard_map/all_gather | solution.py:58
  230.1 3.8 %collective-permute-start.17 = (f32[1,256]{1,0:T(1,128)S(1)}, f32[1,256]{1,0:T(1,128)S(1)}, u32[]{:S(2)}, u32[]{:S(2)}) collective-permute-start(f32[1,256]{1,0:T(1,128)S(1)} %get-tuple-element.76), channel_id=1, source_target_pairs={{0,8},{8,16},{16,24},{1,9},{9,17},{17,25},{2,10},{10,18},{18,26},{... | collective-permute-start | bytes 3080 | tf_op jit(solution)/shard_map/ppermute | solution.py:17
  234.0 1.7 gather_fusion.4
  235.7 2.9 collective-permute-start.16
  238.6 1.7 collective-permute-start.14
  240.3 1.9 collective-permute-done.14
  242.2 1.8 collective-permute-done.15
  244.9 42.0 %all-reduce = (f32[]{:T(128)}, f32[]{:T(128)}) all-reduce(f32[]{:T(128)} %get-tuple-element.56, f32[]{:T(128)} %get-tuple-element.55), channel_id=1, replica_groups=mesh['lat'=4,'lon'=8] {'lat','lon'}, use_global_device_ids=true, to_apply=%region_13.15 | all-reduce | flops 2 | bytes 16 | tf_op jit(solution)/shard_map/psum | solution.py:35
  (70 shorter events, 9.2 us)
Async XLA Ops:
  0.6 1.0 copy-start.4
  1.6 35.0 %collective-permute-start.1 = (f32[128,1]{1,0:T(8,128)S(1)}, f32[128,1]{1,0:T(8,128)S(1)}, u32[]{:S(2)}, u32[]{:S(2)}) collective-permute-start(f32[128,1]{1,0:T(8,128)S(1)} %slice.203), channel_id=1, source_target_pairs={{0,1},{1,2},{2,3},{3,4},{4,5},{5,6},{6,7},{7,0},{8,9},{9,10},{10,1... | collective-permute-start | bytes 1544 | tf_op jit(solution)/shard_map/ppermute | solution.py:17
  1.7 3.5 %copy-start = (s32[128,256]{1,0:T(8,128)S(1)}, s32[128,256]{1,0:T(8,128)}, u32[]{:S(2)}) copy-start(s32[128,256]{1,0:T(8,128)} %param.20) | copy-start | bytes 393220
  1.7 3.5 %copy-start.1 = (f32[128,256]{1,0:T(8,128)S(1)}, f32[128,256]{1,0:T(8,128)}, u32[]{:S(2)}) copy-start(f32[128,256]{1,0:T(8,128)} %param.16) | copy-start | bytes 393220
  1.8 38.5 %collective-permute-start.4 = (f32[1,256]{1,0:T(1,128)S(1)}, f32[1,256]{1,0:T(1,128)S(1)}, u32[]{:S(2)}, u32[]{:S(2)}) collective-permute-start(f32[1,256]{1,0:T(1,128)S(1)} %slice.255), channel_id=1, source_target_pairs={{0,8},{8,16},{16,24},{1,9},{9,17},{17,25},{2,10},{10,18},{18,26},{... | collective-permute-start | bytes 3080 | tf_op jit(solution)/shard_map/ppermute | solution.py:17
  5.3 35.0 %collective-permute-start.3 = (f32[1,256]{1,0:T(1,128)S(1)}, f32[1,256]{1,0:T(1,128)S(1)}, u32[]{:S(2)}, u32[]{:S(2)}) collective-permute-start(f32[1,256]{1,0:T(1,128)S(1)} %get-tuple-element.87), channel_id=1, source_target_pairs={{8,0},{16,8},{24,16},{9,1},{17,9},{25,17},{10,2},{18,10},{26,18},{... | collective-permute-start | bytes 3080 | tf_op jit(solution)/shard_map/ppermute | solution.py:19
  8.6 31.7 %collective-permute-start.5 = (f32[1,256]{1,0:T(1,128)S(1)}, f32[1,256]{1,0:T(1,128)S(1)}, u32[]{:S(2)}, u32[]{:S(2)}) collective-permute-start(f32[1,256]{1,0:T(1,128)S(1)} %get-tuple-element.88), channel_id=1, source_target_pairs={{0,8},{8,16},{16,24},{1,9},{9,17},{17,25},{2,10},{10,18},{18,26},{... | collective-permute-start | bytes 3080 | tf_op jit(solution)/shard_map/ppermute | solution.py:17
  11.2 25.8 %collective-permute-start = (f32[128,1]{1,0:T(8,128)S(1)}, f32[128,1]{1,0:T(8,128)S(1)}, u32[]{:S(2)}, u32[]{:S(2)}) collective-permute-start(f32[128,1]{1,0:T(8,128)S(1)} %get-tuple-element.85), channel_id=1, source_target_pairs={{1,0},{2,1},{3,2},{4,3},{5,4},{6,5},{7,6},{0,7},{9,8},{10,9},{11,1... | collective-permute-start | bytes 1544 | tf_op jit(solution)/shard_map/ppermute | solution.py:19
  12.1 10.8 %copy-start.5 = (s32[256]{0:T(256)S(1)}, s32[256]{0:T(256)}, u32[]{:S(2)}) copy-start(s32[256]{0:T(256)} %param.21) | copy-start | bytes 3076
  34.8 5.5 %copy-start.3 = (f32[128,256]{1,0:T(8,128)S(1)}, f32[128,256]{1,0:T(8,128)}, u32[]{:S(2)}) copy-start(f32[128,256]{1,0:T(8,128)} %param.18) | copy-start | bytes 393220
  36.6 3.7 %collective-permute-start.2 = (f32[128,1]{1,0:T(8,128)S(1)}, f32[128,1]{1,0:T(8,128)S(1)}, u32[]{:S(2)}, u32[]{:S(2)}) collective-permute-start(f32[128,1]{1,0:T(8,128)S(1)} %get-tuple-element.86), channel_id=1, source_target_pairs={{0,1},{1,2},{2,3},{3,4},{4,5},{5,6},{6,7},{7,0},{8,9},{9,10},{10,1... | collective-permute-start | bytes 1544 | tf_op jit(solution)/shard_map/ppermute | solution.py:17
  37.0 3.6 %copy-start.2 = (f32[128,256]{1,0:T(8,128)S(1)}, f32[128,256]{1,0:T(8,128)}, u32[]{:S(2)}) copy-start(f32[128,256]{1,0:T(8,128)} %param.17) | copy-start | bytes 393220
  92.4 13.8 %collective-permute-start.9 = (f32[1,256]{1,0:T(1,128)S(1)}, f32[1,256]{1,0:T(1,128)S(1)}, u32[]{:S(2)}, u32[]{:S(2)}) collective-permute-start(f32[1,256]{1,0:T(1,128)S(1)} %get-tuple-element.84), channel_id=1, source_target_pairs={{0,8},{8,16},{16,24},{1,9},{9,17},{17,25},{2,10},{10,18},{18,26},{... | collective-permute-start | bytes 3080 | tf_op jit(solution)/shard_map/ppermute | solution.py:17
  98.1 8.1 %collective-permute-start.8 = (f32[1,256]{1,0:T(1,128)S(1)}, f32[1,256]{1,0:T(1,128)S(1)}, u32[]{:S(2)}, u32[]{:S(2)}) collective-permute-start(f32[1,256]{1,0:T(1,128)S(1)} %get-tuple-element.83), channel_id=1, source_target_pairs={{8,0},{16,8},{24,16},{9,1},{17,9},{25,17},{10,2},{18,10},{26,18},{... | collective-permute-start | bytes 3080 | tf_op jit(solution)/shard_map/ppermute | solution.py:19
  101.0 3.4 %collective-permute-start.6 = (f32[128,1]{1,0:T(8,128)S(1)}, f32[128,1]{1,0:T(8,128)S(1)}, u32[]{:S(2)}, u32[]{:S(2)}) collective-permute-start(f32[128,1]{1,0:T(8,128)S(1)} %get-tuple-element.81), channel_id=1, source_target_pairs={{1,0},{2,1},{3,2},{4,3},{5,4},{6,5},{7,6},{0,7},{9,8},{10,9},{11,1... | collective-permute-start | bytes 1544 | tf_op jit(solution)/shard_map/ppermute | solution.py:19
  102.5 3.7 %collective-permute-start.7 = (f32[128,1]{1,0:T(8,128)S(1)}, f32[128,1]{1,0:T(8,128)S(1)}, u32[]{:S(2)}, u32[]{:S(2)}) collective-permute-start(f32[128,1]{1,0:T(8,128)S(1)} %get-tuple-element.82), channel_id=1, source_target_pairs={{0,1},{1,2},{2,3},{3,4},{4,5},{5,6},{6,7},{7,0},{8,9},{9,10},{10,1... | collective-permute-start | bytes 1544 | tf_op jit(solution)/shard_map/ppermute | solution.py:17
  162.0 14.0 %collective-permute-start.13 = (f32[1,256]{1,0:T(1,128)S(1)}, f32[1,256]{1,0:T(1,128)S(1)}, u32[]{:S(2)}, u32[]{:S(2)}) collective-permute-start(f32[1,256]{1,0:T(1,128)S(1)} %get-tuple-element.80), channel_id=1, source_target_pairs={{0,8},{8,16},{16,24},{1,9},{9,17},{17,25},{2,10},{10,18},{18,26},{... | collective-permute-start | bytes 3080 | tf_op jit(solution)/shard_map/ppermute | solution.py:17
  166.6 9.4 %collective-permute-start.12 = (f32[1,256]{1,0:T(1,128)S(1)}, f32[1,256]{1,0:T(1,128)S(1)}, u32[]{:S(2)}, u32[]{:S(2)}) collective-permute-start(f32[1,256]{1,0:T(1,128)S(1)} %get-tuple-element.79), channel_id=1, source_target_pairs={{8,0},{16,8},{24,16},{9,1},{17,9},{25,17},{10,2},{18,10},{26,18},{... | collective-permute-start | bytes 3080 | tf_op jit(solution)/shard_map/ppermute | solution.py:19
  170.6 3.6 %collective-permute-start.10 = (f32[128,1]{1,0:T(8,128)S(1)}, f32[128,1]{1,0:T(8,128)S(1)}, u32[]{:S(2)}, u32[]{:S(2)}) collective-permute-start(f32[128,1]{1,0:T(8,128)S(1)} %get-tuple-element.77), channel_id=1, source_target_pairs={{1,0},{2,1},{3,2},{4,3},{5,4},{6,5},{7,6},{0,7},{9,8},{10,9},{11,1... | collective-permute-start | bytes 1544 | tf_op jit(solution)/shard_map/ppermute | solution.py:19
  172.3 3.7 %collective-permute-start.11 = (f32[128,1]{1,0:T(8,128)S(1)}, f32[128,1]{1,0:T(8,128)S(1)}, u32[]{:S(2)}, u32[]{:S(2)}) collective-permute-start(f32[128,1]{1,0:T(8,128)S(1)} %get-tuple-element.78), channel_id=1, source_target_pairs={{0,1},{1,2},{2,3},{3,4},{4,5},{5,6},{6,7},{7,0},{8,9},{9,10},{10,1... | collective-permute-start | bytes 1544 | tf_op jit(solution)/shard_map/ppermute | solution.py:17
  230.1 13.9 %collective-permute-start.17 = (f32[1,256]{1,0:T(1,128)S(1)}, f32[1,256]{1,0:T(1,128)S(1)}, u32[]{:S(2)}, u32[]{:S(2)}) collective-permute-start(f32[1,256]{1,0:T(1,128)S(1)} %get-tuple-element.76), channel_id=1, source_target_pairs={{0,8},{8,16},{16,24},{1,9},{9,17},{17,25},{2,10},{10,18},{18,26},{... | collective-permute-start | bytes 3080 | tf_op jit(solution)/shard_map/ppermute | solution.py:17
  235.7 8.3 %collective-permute-start.16 = (f32[1,256]{1,0:T(1,128)S(1)}, f32[1,256]{1,0:T(1,128)S(1)}, u32[]{:S(2)}, u32[]{:S(2)}) collective-permute-start(f32[1,256]{1,0:T(1,128)S(1)} %get-tuple-element.75), channel_id=1, source_target_pairs={{8,0},{16,8},{24,16},{9,1},{17,9},{25,17},{10,2},{18,10},{26,18},{... | collective-permute-start | bytes 3080 | tf_op jit(solution)/shard_map/ppermute | solution.py:19
  238.6 3.6 %collective-permute-start.14 = (f32[128,1]{1,0:T(8,128)S(1)}, f32[128,1]{1,0:T(8,128)S(1)}, u32[]{:S(2)}, u32[]{:S(2)}) collective-permute-start(f32[128,1]{1,0:T(8,128)S(1)} %get-tuple-element.73), channel_id=1, source_target_pairs={{1,0},{2,1},{3,2},{4,3},{5,4},{6,5},{7,6},{0,7},{9,8},{10,9},{11,1... | collective-permute-start | bytes 1544 | tf_op jit(solution)/shard_map/ppermute | solution.py:19
  240.3 3.7 %collective-permute-start.15 = (f32[128,1]{1,0:T(8,128)S(1)}, f32[128,1]{1,0:T(8,128)S(1)}, u32[]{:S(2)}, u32[]{:S(2)}) collective-permute-start(f32[128,1]{1,0:T(8,128)S(1)} %get-tuple-element.74), channel_id=1, source_target_pairs={{0,1},{1,2},{2,3},{3,4},{4,5},{5,6},{6,7},{7,0},{8,9},{9,10},{10,1... | collective-permute-start | bytes 1544 | tf_op jit(solution)/shard_map/ppermute | solution.py:17
where the time goes:
time: 293 us; the launch traced here: 292 us
  blocking collectives  212 us (72%)
  starting transfers between devices  35.7 us (12%)
  between operations  14.9 us (5%)
  waiting for transfers between devices  14.4 us (5%)
  local copies, waits for them, and re-layouts  10.1 us (3%)
  other arithmetic  4.81 us (2%)
    psum x4, blocking collectives, paired(): lax.psum((jnp.sum(residual * residual), jnp.sum(residual * image)), ('lat...  166 us
    all_gather x5, blocking collectives, mirror_row(): whole_row = lax.all_gather(top_values, 'lon', axis=0, tiled=True)  45.7 us
    ppermute x8, starting transfers between devices, with_halo(): lax.ppermute(head, axis, [((i + 1) % count, i) for i in range(ends)])  18.9 us
    ppermute x10, starting transfers between devices, with_halo(): lax.ppermute(tail, axis, [(i, (i + 1) % count) for i in range(ends)])  16.8 us
    ppermute x10, waiting for transfers between devices, with_halo(): lax.ppermute(tail, axis, [(i, (i + 1) % count) for i in range(ends)])  8.69 us
    gather x5, local copies, waits for them, and re-layouts, mirror_row(): return jnp.take(whole_row, fold_partner, axis=0)  8.62 us
  transfers between devices with their start and end apart: 18, of which 7 were waited for; matrix products, arithmetic and copies ran while one was open for 3% of the time, Pallas kernels for 0%

commit v1 on v0

--- a/solution.py
+++ b/solution.py
@@ -32,7 +32,9 @@
 
 
 def paired(residual, image):
-    return lax.psum((jnp.sum(residual * residual), jnp.sum(residual * image)), ("lat", "lon"))
+    return lax.psum(
+        lax.psum((jnp.sum(residual * residual), jnp.sum(residual * image)), "lon"), "lat"
+    )
 
 
 def local(right_side, diagonal, east_coef, north_coef, land_sea, fold_partner):

time: 293 us -> 230 us (0.78)
  the two profiles are of different devices: /device:TPU:12 before, /device:TPU:0 now
where the time goes in v1:
time: 230 us
  blocking collectives  148 us (64%)
  starting transfers between devices  30.4 us (13%)
  waiting for transfers between devices  21.6 us (9%)
  between operations  14.6 us (6%)
  local copies, waits for them, and re-layouts  10.1 us (4%)
  other arithmetic  4.8 us (2%)
    psum x4, blocking collectives, paired(): lax.psum((jnp.sum(residual * residual), jnp.sum(residual * image)), 'lon')  58.8 us
    psum x4, blocking collectives, paired(): lax.psum(lax.psum((jnp.sum(residual * residual), jnp.sum(residual * image...  45 us
    all_gather x5, blocking collectives, mirror_row(): whole_row = lax.all_gather(top_values, 'lon', axis=0, tiled=True)  44.4 us
    ppermute x10, starting transfers between devices, with_halo(): lax.ppermute(tail, axis, [(i, (i + 1) % count) for i in range(ends)])  17.4 us
    ppermute x10, waiting for transfers between devices, with_halo(): lax.ppermute(tail, axis, [(i, (i + 1) % count) for i in range(ends)])  14.7 us
    ppermute x8, starting transfers between devices, with_halo(): lax.ppermute(head, axis, [((i + 1) % count, i) for i in range(ends)])  13 us
    gather x5, local copies, waits for them, and re-layouts, mirror_row(): return jnp.take(whole_row, fold_partner, axis=0)  8.62 us
    ppermute x8, waiting for transfers between devices, with_halo(): lax.ppermute(head, axis, [((i + 1) % count, i) for i in range(ends)])  6.88 us
  transfers between devices with their start and end apart: 18, of which 7 were waited for; matrix products, arithmetic and copies ran while one was open for 4% of the time, Pallas kernels for 0%

profile of v1, /device:TPU:0, one launch (start us, length us, event | category | flops | bytes accessed | tf_op | source)
XLA Modules:
  0.0 229.7 jit_solution(18013462143507745809)
XLA Ops:
  2.3 4.4 %collective-permute-start.4 = (f32[1,256]{1,0:T(1,128)S(1)}, f32[1,256]{1,0:T(1,128)S(1)}, u32[]{:S(2)}, u32[]{:S(2)}) collective-permute-start(f32[1,256]{1,0:T(1,128)S(1)} %slice.255), channel_id=1, source_target_pairs={{0,8},{8,16},{16,24},{1,9},{9,17},{17,25},{2,10},{10,18},{18,26},{... | collective-permute-start | bytes 3080 | tf_op jit(solution)/shard_map/ppermute | solution.py:17
  8.0 4.5 %collective-permute-start.5 = (f32[1,256]{1,0:T(1,128)S(1)}, f32[1,256]{1,0:T(1,128)S(1)}, u32[]{:S(2)}, u32[]{:S(2)}) collective-permute-start(f32[1,256]{1,0:T(1,128)S(1)} %get-tuple-element.96), channel_id=1, source_target_pairs={{0,8},{8,16},{16,24},{1,9},{9,17},{17,25},{2,10},{10,18},{18,26},{... | collective-permute-start | bytes 3080 | tf_op jit(solution)/shard_map/ppermute | solution.py:17
  12.7 2.7 %collective-permute-start = (f32[128,1]{1,0:T(8,128)S(1)}, f32[128,1]{1,0:T(8,128)S(1)}, u32[]{:S(2)}, u32[]{:S(2)}) collective-permute-start(f32[128,1]{1,0:T(8,128)S(1)} %get-tuple-element.93), channel_id=1, source_target_pairs={{1,0},{2,1},{3,2},{4,3},{5,4},{6,5},{7,6},{0,7},{9,8},{10,9},{11,1... | collective-permute-start | bytes 1544 | tf_op jit(solution)/shard_map/ppermute | solution.py:19
  15.4 10.3 %all-gather.1 = f32[1,2048]{1,0:T(1,128)S(1)} all-gather(f32[1,256]{1,0:T(1,128)S(1)} %get-tuple-element.96), channel_id=3, replica_groups=mesh['lat'=4,'lon'=8] {'lon'}, dimensions={1}, use_global_device_ids=true | all-gather | bytes 9216 | tf_op jit(solution)/shard_map/all_gather | solution.py:60
  25.7 8.8 %all-gather = f32[1,2048]{1,0:T(1,128)S(1)} all-gather(f32[1,256]{1,0:T(1,128)S(1)} %slice.214), channel_id=2, replica_groups=mesh['lat'=4,'lon'=8] {'lon'}, dimensions={1}, use_global_device_ids=true | all-gather | bytes 9216 | tf_op jit(solution)/shard_map/all_gather | solution.py:60
  34.5 1.7 gather_fusion
  36.2 1.7 gather_fusion.1
  38.4 5.1 %collective-permute-done.2 = f32[128,1]{1,0:T(8,128)S(1)} collective-permute-done((f32[128,1]{1,0:T(8,128)S(1)}, f32[128,1]{1,0:T(8,128)S(1)}, u32[]{:S(2)}, u32[]{:S(2)}) %collective-permute-start.2) | collective-permute-done | bytes 544 | tf_op jit(solution)/shard_map/ppermute | solution.py:17
  44.4 14.2 %all-reduce.3 = (f32[]{:T(128)}, f32[]{:T(128)}) all-reduce(f32[]{:T(128)} %get-tuple-element.58, f32[]{:T(128)} %get-tuple-element.57), channel_id=1, replica_groups=mesh['lat'=4,'lon'=8] {'lon'}, use_global_device_ids=true, to_apply=%region_1.2 | all-reduce | flops 2 | bytes 16 | tf_op jit(solution)/shard_map/psum | solution.py:36
  58.6 10.5 %all-reduce.7 = (f32[]{:T(128)}, f32[]{:T(128)}) all-reduce(f32[]{:T(128)} %get-tuple-element.65, f32[]{:T(128)} %get-tuple-element.66), channel_id=1, replica_groups=mesh['lat'=4,'lon'=8] {'lat'}, use_global_device_ids=true, to_apply=%region_2.3 | all-reduce | flops 2 | bytes 16 | tf_op jit(solution)/shard_map/psum | solution.py:35
  70.5 8.4 %all-gather.2 = f32[1,2048]{1,0:T(1,128)S(1)} all-gather(f32[1,256]{1,0:T(1,128)S(1)} %get-tuple-element.92), channel_id=4, replica_groups=mesh['lat'=4,'lon'=8] {'lon'}, dimensions={1}, use_global_device_ids=true | all-gather | bytes 9216 | tf_op jit(solution)/shard_map/all_gather | solution.py:60
  80.7 1.7 gather_fusion.2
  83.7 1.7 collective-permute-start.6
  85.4 2.3 collective-permute-done.6
  87.7 3.2 %collective-permute-done.7 = f32[128,1]{1,0:T(8,128)S(1)} collective-permute-done((f32[128,1]{1,0:T(8,128)S(1)}, f32[128,1]{1,0:T(8,128)S(1)}, u32[]{:S(2)}, u32[]{:S(2)}) %collective-permute-start.7) | collective-permute-done | bytes 544 | tf_op jit(solution)/shard_map/ppermute | solution.py:17
  91.9 14.9 %all-reduce.2 = (f32[]{:T(128)}, f32[]{:T(128)}) all-reduce(f32[]{:T(128)} %get-tuple-element.54, f32[]{:T(128)} %get-tuple-element.53), channel_id=1, replica_groups=mesh['lat'=4,'lon'=8] {'lon'}, use_global_device_ids=true, to_apply=%region_7.9 | all-reduce | flops 2 | bytes 16 | tf_op jit(solution)/shard_map/psum | solution.py:36
  106.8 11.9 %all-reduce.6 = (f32[]{:T(128)}, f32[]{:T(128)}) all-reduce(f32[]{:T(128)} %get-tuple-element.63, f32[]{:T(128)} %get-tuple-element.64), channel_id=1, replica_groups=mesh['lat'=4,'lon'=8] {'lat'}, use_global_device_ids=true, to_apply=%region_8.10 | all-reduce | flops 2 | bytes 16 | tf_op jit(solution)/shard_map/psum | solution.py:35
  123.4 8.4 %all-gather.3 = f32[1,2048]{1,0:T(1,128)S(1)} all-gather(f32[1,256]{1,0:T(1,128)S(1)} %get-tuple-element.88), channel_id=5, replica_groups=mesh['lat'=4,'lon'=8] {'lon'}, dimensions={1}, use_global_device_ids=true | all-gather | bytes 9216 | tf_op jit(solution)/shard_map/all_gather | solution.py:60
  131.9 3.6 %collective-permute-start.13 = (f32[1,256]{1,0:T(1,128)S(1)}, f32[1,256]{1,0:T(1,128)S(1)}, u32[]{:S(2)}, u32[]{:S(2)}) collective-permute-start(f32[1,256]{1,0:T(1,128)S(1)} %get-tuple-element.88), channel_id=1, source_target_pairs={{0,8},{8,16},{16,24},{1,9},{9,17},{17,25},{2,10},{10,18},{18,26},{... | collective-permute-start | bytes 3080 | tf_op jit(solution)/shard_map/ppermute | solution.py:17
  135.6 1.7 gather_fusion.3
  138.6 1.7 collective-permute-start.10
  140.3 2.3 collective-permute-done.10
  142.6 3.2 %collective-permute-done.11 = f32[128,1]{1,0:T(8,128)S(1)} collective-permute-done((f32[128,1]{1,0:T(8,128)S(1)}, f32[128,1]{1,0:T(8,128)S(1)}, u32[]{:S(2)}, u32[]{:S(2)}) %collective-permute-start.11) | collective-permute-done | bytes 544 | tf_op jit(solution)/shard_map/ppermute | solution.py:17
  146.8 14.8 %all-reduce.1 = (f32[]{:T(128)}, f32[]{:T(128)}) all-reduce(f32[]{:T(128)} %get-tuple-element.52, f32[]{:T(128)} %get-tuple-element.51), channel_id=1, replica_groups=mesh['lat'=4,'lon'=8] {'lon'}, use_global_device_ids=true, to_apply=%region_13.15 | all-reduce | flops 2 | bytes 16 | tf_op jit(solution)/shard_map/psum | solution.py:36
  161.6 11.3 %all-reduce.5 = (f32[]{:T(128)}, f32[]{:T(128)}) all-reduce(f32[]{:T(128)} %get-tuple-element.61, f32[]{:T(128)} %get-tuple-element.62), channel_id=1, replica_groups=mesh['lat'=4,'lon'=8] {'lat'}, use_global_device_ids=true, to_apply=%region_14.16 | all-reduce | flops 2 | bytes 16 | tf_op jit(solution)/shard_map/psum | solution.py:35
  177.0 8.4 %all-gather.4 = f32[1,2048]{1,0:T(1,128)S(1)} all-gather(f32[1,256]{1,0:T(1,128)S(1)} %get-tuple-element.84), channel_id=6, replica_groups=mesh['lat'=4,'lon'=8] {'lon'}, dimensions={1}, use_global_device_ids=true | all-gather | bytes 9216 | tf_op jit(solution)/shard_map/all_gather | solution.py:60
  185.4 2.2 collective-permute-start.17
  187.8 1.7 gather_fusion.4
  192.5 2.3 collective-permute-done.14
  194.8 3.2 %collective-permute-done.15 = f32[128,1]{1,0:T(8,128)S(1)} collective-permute-done((f32[128,1]{1,0:T(8,128)S(1)}, f32[128,1]{1,0:T(8,128)S(1)}, u32[]{:S(2)}, u32[]{:S(2)}) %collective-permute-start.15) | collective-permute-done | bytes 544 | tf_op jit(solution)/shard_map/ppermute | solution.py:17
  198.9 14.9 %all-reduce = (f32[]{:T(128)}, f32[]{:T(128)}) all-reduce(f32[]{:T(128)} %get-tuple-element.56, f32[]{:T(128)} %get-tuple-element.55), channel_id=1, replica_groups=mesh['lat'=4,'lon'=8] {'lon'}, use_global_device_ids=true, to_apply=%region_19.21 | all-reduce | flops 2 | bytes 16 | tf_op jit(solution)/shard_map/psum | solution.py:36
  213.8 11.3 %all-reduce.4 = (f32[]{:T(128)}, f32[]{:T(128)}) all-reduce(f32[]{:T(128)} %get-tuple-element.59, f32[]{:T(128)} %get-tuple-element.60), channel_id=1, replica_groups=mesh['lat'=4,'lon'=8] {'lat'}, use_global_device_ids=true, to_apply=%region_20.22 | all-reduce | flops 2 | bytes 16 | tf_op jit(solution)/shard_map/psum | solution.py:35
  (74 shorter events, 15.8 us)
Async XLA Ops:
  0.6 1.5 copy-start.4
  1.6 36.3 %collective-permute-start.1 = (f32[128,1]{1,0:T(8,128)S(1)}, f32[128,1]{1,0:T(8,128)S(1)}, u32[]{:S(2)}, u32[]{:S(2)}) collective-permute-start(f32[128,1]{1,0:T(8,128)S(1)} %slice.203), channel_id=1, source_target_pairs={{0,1},{1,2},{2,3},{3,4},{4,5},{5,6},{6,7},{7,0},{8,9},{9,10},{10,1... | collective-permute-start | bytes 1544 | tf_op jit(solution)/shard_map/ppermute | solution.py:17
  2.1 4.5 %copy-start = (s32[128,256]{1,0:T(8,128)S(1)}, s32[128,256]{1,0:T(8,128)}, u32[]{:S(2)}) copy-start(s32[128,256]{1,0:T(8,128)} %param.20) | copy-start | bytes 393220
  2.1 4.6 %copy-start.1 = (f32[128,256]{1,0:T(8,128)S(1)}, f32[128,256]{1,0:T(8,128)}, u32[]{:S(2)}) copy-start(f32[128,256]{1,0:T(8,128)} %param.16) | copy-start | bytes 393220
  2.3 41.2 %collective-permute-start.4 = (f32[1,256]{1,0:T(1,128)S(1)}, f32[1,256]{1,0:T(1,128)S(1)}, u32[]{:S(2)}, u32[]{:S(2)}) collective-permute-start(f32[1,256]{1,0:T(1,128)S(1)} %slice.255), channel_id=1, source_target_pairs={{0,8},{8,16},{16,24},{1,9},{9,17},{17,25},{2,10},{10,18},{18,26},{... | collective-permute-start | bytes 3080 | tf_op jit(solution)/shard_map/ppermute | solution.py:17
  6.7 36.7 %collective-permute-start.3 = (f32[1,256]{1,0:T(1,128)S(1)}, f32[1,256]{1,0:T(1,128)S(1)}, u32[]{:S(2)}, u32[]{:S(2)}) collective-permute-start(f32[1,256]{1,0:T(1,128)S(1)} %get-tuple-element.95), channel_id=1, source_target_pairs={{8,0},{16,8},{24,16},{9,1},{17,9},{25,17},{10,2},{18,10},{26,18},{... | collective-permute-start | bytes 3080 | tf_op jit(solution)/shard_map/ppermute | solution.py:19
  8.0 35.5 %collective-permute-start.5 = (f32[1,256]{1,0:T(1,128)S(1)}, f32[1,256]{1,0:T(1,128)S(1)}, u32[]{:S(2)}, u32[]{:S(2)}) collective-permute-start(f32[1,256]{1,0:T(1,128)S(1)} %get-tuple-element.96), channel_id=1, source_target_pairs={{0,8},{8,16},{16,24},{1,9},{9,17},{17,25},{2,10},{10,18},{18,26},{... | collective-permute-start | bytes 3080 | tf_op jit(solution)/shard_map/ppermute | solution.py:17
  12.7 25.7 %collective-permute-start = (f32[128,1]{1,0:T(8,128)S(1)}, f32[128,1]{1,0:T(8,128)S(1)}, u32[]{:S(2)}, u32[]{:S(2)}) collective-permute-start(f32[128,1]{1,0:T(8,128)S(1)} %get-tuple-element.93), channel_id=1, source_target_pairs={{1,0},{2,1},{3,2},{4,3},{5,4},{6,5},{7,6},{0,7},{9,8},{10,9},{11,1... | collective-permute-start | bytes 1544 | tf_op jit(solution)/shard_map/ppermute | solution.py:19
  15.4 10.3 %copy-start.5 = (s32[256]{0:T(256)S(1)}, s32[256]{0:T(256)}, u32[]{:S(2)}) copy-start(s32[256]{0:T(256)} %param.21) | copy-start | bytes 3076
  36.2 7.3 %copy-start.3 = (f32[128,256]{1,0:T(8,128)S(1)}, f32[128,256]{1,0:T(8,128)}, u32[]{:S(2)}) copy-start(f32[128,256]{1,0:T(8,128)} %param.18) | copy-start | bytes 393220
  37.9 5.5 %collective-permute-start.2 = (f32[128,1]{1,0:T(8,128)S(1)}, f32[128,1]{1,0:T(8,128)S(1)}, u32[]{:S(2)}, u32[]{:S(2)}) collective-permute-start(f32[128,1]{1,0:T(8,128)S(1)} %get-tuple-element.94), channel_id=1, source_target_pairs={{0,1},{1,2},{2,3},{3,4},{4,5},{5,6},{6,7},{7,0},{8,9},{9,10},{10,1... | collective-permute-start | bytes 1544 | tf_op jit(solution)/shard_map/ppermute | solution.py:17
  38.3 5.4 %copy-start.2 = (f32[128,256]{1,0:T(8,128)S(1)}, f32[128,256]{1,0:T(8,128)}, u32[]{:S(2)}) copy-start(f32[128,256]{1,0:T(8,128)} %param.17) | copy-start | bytes 393220
  79.0 12.0 %collective-permute-start.9 = (f32[1,256]{1,0:T(1,128)S(1)}, f32[1,256]{1,0:T(1,128)S(1)}, u32[]{:S(2)}, u32[]{:S(2)}) collective-permute-start(f32[1,256]{1,0:T(1,128)S(1)} %get-tuple-element.92), channel_id=1, source_target_pairs={{0,8},{8,16},{16,24},{1,9},{9,17},{17,25},{2,10},{10,18},{18,26},{... | collective-permute-start | bytes 3080 | tf_op jit(solution)/shard_map/ppermute | solution.py:17
  82.4 8.5 %collective-permute-start.8 = (f32[1,256]{1,0:T(1,128)S(1)}, f32[1,256]{1,0:T(1,128)S(1)}, u32[]{:S(2)}, u32[]{:S(2)}) collective-permute-start(f32[1,256]{1,0:T(1,128)S(1)} %get-tuple-element.91), channel_id=1, source_target_pairs={{8,0},{16,8},{24,16},{9,1},{17,9},{25,17},{10,2},{18,10},{26,18},{... | collective-permute-start | bytes 3080 | tf_op jit(solution)/shard_map/ppermute | solution.py:19
  83.7 4.0 %collective-permute-start.6 = (f32[128,1]{1,0:T(8,128)S(1)}, f32[128,1]{1,0:T(8,128)S(1)}, u32[]{:S(2)}, u32[]{:S(2)}) collective-permute-start(f32[128,1]{1,0:T(8,128)S(1)} %get-tuple-element.89), channel_id=1, source_target_pairs={{1,0},{2,1},{3,2},{4,3},{5,4},{6,5},{7,6},{0,7},{9,8},{10,9},{11,1... | collective-permute-start | bytes 1544 | tf_op jit(solution)/shard_map/ppermute | solution.py:19
  85.4 5.5 %collective-permute-start.7 = (f32[128,1]{1,0:T(8,128)S(1)}, f32[128,1]{1,0:T(8,128)S(1)}, u32[]{:S(2)}, u32[]{:S(2)}) collective-permute-start(f32[128,1]{1,0:T(8,128)S(1)} %get-tuple-element.90), channel_id=1, source_target_pairs={{0,1},{1,2},{2,3},{3,4},{4,5},{5,6},{6,7},{7,0},{8,9},{9,10},{10,1... | collective-permute-start | bytes 1544 | tf_op jit(solution)/shard_map/ppermute | solution.py:17
  131.9 13.9 %collective-permute-start.13 = (f32[1,256]{1,0:T(1,128)S(1)}, f32[1,256]{1,0:T(1,128)S(1)}, u32[]{:S(2)}, u32[]{:S(2)}) collective-permute-start(f32[1,256]{1,0:T(1,128)S(1)} %get-tuple-element.88), channel_id=1, source_target_pairs={{0,8},{8,16},{16,24},{1,9},{9,17},{17,25},{2,10},{10,18},{18,26},{... | collective-permute-start | bytes 3080 | tf_op jit(solution)/shard_map/ppermute | solution.py:17
  137.3 8.5 %collective-permute-start.12 = (f32[1,256]{1,0:T(1,128)S(1)}, f32[1,256]{1,0:T(1,128)S(1)}, u32[]{:S(2)}, u32[]{:S(2)}) collective-permute-start(f32[1,256]{1,0:T(1,128)S(1)} %get-tuple-element.87), channel_id=1, source_target_pairs={{8,0},{16,8},{24,16},{9,1},{17,9},{25,17},{10,2},{18,10},{26,18},{... | collective-permute-start | bytes 3080 | tf_op jit(solution)/shard_map/ppermute | solution.py:19
  138.6 4.0 %collective-permute-start.10 = (f32[128,1]{1,0:T(8,128)S(1)}, f32[128,1]{1,0:T(8,128)S(1)}, u32[]{:S(2)}, u32[]{:S(2)}) collective-permute-start(f32[128,1]{1,0:T(8,128)S(1)} %get-tuple-element.85), channel_id=1, source_target_pairs={{1,0},{2,1},{3,2},{4,3},{5,4},{6,5},{7,6},{0,7},{9,8},{10,9},{11,1... | collective-permute-start | bytes 1544 | tf_op jit(solution)/shard_map/ppermute | solution.py:19
  140.3 5.5 %collective-permute-start.11 = (f32[128,1]{1,0:T(8,128)S(1)}, f32[128,1]{1,0:T(8,128)S(1)}, u32[]{:S(2)}, u32[]{:S(2)}) collective-permute-start(f32[128,1]{1,0:T(8,128)S(1)} %get-tuple-element.86), channel_id=1, source_target_pairs={{0,1},{1,2},{2,3},{3,4},{4,5},{5,6},{6,7},{7,0},{8,9},{9,10},{10,1... | collective-permute-start | bytes 1544 | tf_op jit(solution)/shard_map/ppermute | solution.py:17
  185.4 12.6 %collective-permute-start.17 = (f32[1,256]{1,0:T(1,128)S(1)}, f32[1,256]{1,0:T(1,128)S(1)}, u32[]{:S(2)}, u32[]{:S(2)}) collective-permute-start(f32[1,256]{1,0:T(1,128)S(1)} %get-tuple-element.84), channel_id=1, source_target_pairs={{0,8},{8,16},{16,24},{1,9},{9,17},{17,25},{2,10},{10,18},{18,26},{... | collective-permute-start | bytes 3080 | tf_op jit(solution)/shard_map/ppermute | solution.py:17
  189.5 8.5 %collective-permute-start.16 = (f32[1,256]{1,0:T(1,128)S(1)}, f32[1,256]{1,0:T(1,128)S(1)}, u32[]{:S(2)}, u32[]{:S(2)}) collective-permute-start(f32[1,256]{1,0:T(1,128)S(1)} %get-tuple-element.83), channel_id=1, source_target_pairs={{8,0},{16,8},{24,16},{9,1},{17,9},{25,17},{10,2},{18,10},{26,18},{... | collective-permute-start | bytes 3080 | tf_op jit(solution)/shard_map/ppermute | solution.py:19
  190.8 4.0 %collective-permute-start.14 = (f32[128,1]{1,0:T(8,128)S(1)}, f32[128,1]{1,0:T(8,128)S(1)}, u32[]{:S(2)}, u32[]{:S(2)}) collective-permute-start(f32[128,1]{1,0:T(8,128)S(1)} %get-tuple-element.81), channel_id=1, source_target_pairs={{1,0},{2,1},{3,2},{4,3},{5,4},{6,5},{7,6},{0,7},{9,8},{10,9},{11,1... | collective-permute-start | bytes 1544 | tf_op jit(solution)/shard_map/ppermute | solution.py:19
  192.5 5.5 %collective-permute-start.15 = (f32[128,1]{1,0:T(8,128)S(1)}, f32[128,1]{1,0:T(8,128)S(1)}, u32[]{:S(2)}, u32[]{:S(2)}) collective-permute-start(f32[128,1]{1,0:T(8,128)S(1)} %get-tuple-element.82), channel_id=1, source_target_pairs={{0,1},{1,2},{2,3},{3,4},{4,5},{5,6},{6,7},{7,0},{8,9},{9,10},{10,1... | collective-permute-start | bytes 1544 | tf_op jit(solution)/shard_map/ppermute | solution.py:17
